TPU v7x, 256 devices: a whole 4x4x8 slice. The times are simulated.
256 devices in a mesh: scen: 16 (over z, core), clus: 16 (over y, x).
Axes of the slice: x: 4, y: 4, z: 8, core: 2. Of those that a mesh axis runs over, the one named last changes fastest.
Arguments:
- duals: bfloat16 [16384, 2, 128], P(('scen', 'clus')), may hold values from -6 to 6
- blocks: bfloat16 [16384, 2, 128, 128], P(('scen', 'clus')), may hold values from -0.5 to 0.5
- prob: float32 [16384], P(('scen', 'clus')), may hold values from 0.25 to 4
- cluster_map: int32 [16384], P(('scen', 'clus')), may hold values from 0 to 15
- block_cols: int32 [16384, 2], P(('scen', 'clus')), may hold values from 0 to 255
- counts: int32 [256], P(('scen', 'clus')), may hold values from 16 to 64, as said below
- cut_owner_rows: int32 [256], replicated, may hold values from 0 to 255, as said below
Outputs:
- master_cuts: float32 [256, 32768], P('clus', 'scen')
Inputs may be any that keep to these rules, and one draw needn't show every extreme that they name: counts of live slots, one device holding 64 live slots in every draw. A permutation of the master cut rows; of the cuts k = i * 16 to (i + 1) * 16 - 1 at most 1 have cut_owner_rows[k] in e * 16 to (e + 1) * 16 - 1, for any i and e, and 1 is reached.
All inputs are finite; a program needn't handle non-finite values.
Results may differ from a plain program's by a relative error of at most 0.0029.
Values sent between devices are 32-bit elements; how exact they have to be, the bound alone decides.
A program may use at most 64 MiB of HBM per device.

v0:
```python
import jax
import jax.numpy as jnp
from jax import lax
from jax.sharding import PartitionSpec as P

N1 = 32768
KC = 16


def body(duals, blocks, prob, cluster_map, block_cols, counts, cut_owner_rows):
    slots = prob.shape[0]
    width = blocks.shape[-1]
    col_blocks = N1 // width
    cluster_position = lax.axis_index("clus")
    own_blocks = col_blocks // lax.axis_size("scen")
    columns = own_blocks * width
    live = jnp.arange(slots, dtype=jnp.int32) < counts[0]
    weight = jnp.where(live, prob, jnp.float32(0.0))
    weighted_duals = (weight[:, None, None] * duals.astype(jnp.float32)).astype(jnp.bfloat16)
    dual_products = jnp.einsum(
        "plqv,plq->plv", blocks, weighted_duals, preferred_element_type=jnp.float32
    )
    dual_products = dual_products.reshape(-1, width)
    keys = (cluster_map[:, None] * col_blocks + block_cols).reshape(-1)
    clus_part = keys // col_blocks
    col_part = keys % col_blocks
    valid = (col_part >= 0) & (col_part < lax.axis_size("scen") * own_blocks)
    target = jnp.where(valid, col_part * KC + clus_part, -1)
    onehot = (
        target[None, :]
        == jnp.arange(lax.axis_size("scen") * own_blocks * KC, dtype=jnp.int32)[:, None]
    ).astype(jnp.float32)
    summed = jnp.dot(
        onehot, dual_products, precision=lax.Precision.HIGHEST, preferred_element_type=jnp.float32
    )
    probability_shares = lax.psum_scatter(
        summed.reshape(lax.axis_size("scen") * own_blocks, KC, width),
        "scen",
        scatter_dimension=0,
        tiled=True,
    )
    reduced = jnp.transpose(probability_shares, (1, 0, 2)).reshape(KC, columns)
    owners = cut_owner_rows - cluster_position * KC
    onehot = (owners[None, :] == jnp.arange(KC, dtype=jnp.int32)[:, None]).astype(jnp.float32)
    return jnp.dot(
        onehot,
        lax.all_gather(reduced, "clus", axis=0, tiled=True),
        precision=lax.Precision.HIGHEST,
        preferred_element_type=jnp.float32,
    )


def solution(mesh):
    placed = (
        P(("scen", "clus"), None, None),
        P(("scen", "clus"), None, None, None),
        P(("scen", "clus")),
        P(("scen", "clus")),
        P(("scen", "clus"), None),
        P(("scen", "clus")),
        P(),
    )
    return jax.shard_map(
        body, mesh=mesh, in_specs=placed, out_specs=P("clus", "scen"), check_vma=False
    )
```

profile of v0, /device:TPU:1, one launch (start us, length us, event | category | flops | bytes accessed | tf_op | source)
XLA Modules:
  0.0 139.5 jit_solution(1167170672462910426)
XLA Ops:
  6.5 0.0 reduce-scatter.2.cloned.1.call-start
  7.2 0.7 broadcast_multiply_fusion
  7.9 0.7 broadcast_add_fusion
  8.5 0.1 copy.9
  8.6 0.1 reshape.86
  8.8 0.7 compare_select_fusion
  9.5 0.9 fusion.6
  10.3 3.4 %fusion.4 = f32[64,2,1,128]{3,2,1,0:T(1,128)S(1)} fusion(bf16[64,2,128,128]{3,2,1,0:T(8,128)(2,1)} %param.8, bf16[64,2,128,1]{2,1,0,3:T(2,128)(2,1)S(1)} %fusion.6), kind=kOutput, calls=%fused_computation.5 | convolution fusion | flops 4194304 | bytes 4292608 | tf_op jit(solution)/shard_map/plqv,plq->plv/dot_general | solution.py:20
  13.7 0.0 copy-start
  13.7 2.5 %fusion = f32[256,16,128]{2,0,1:T(8,128)} fusion(f32[128,128,1]{1,0,2:T(8,128)S(1)} %bitcast.19, s32[256,16]{0,1:T(8,128)S(1)} %multiply_add_fusion, s32[128]{0:T(128)S(1)} %and_select_fusion.1), kind=kOutput, calls=%fused_computation | convolution fusion | flops 805830656 | bytes 2179584 | tf_op jit(solution)/shard_map/dot_general | solution.py:33
  16.2 0.0 reduce-scatter.2.cloned.1.call-update
  16.3 0.0 all-gather.2.cloned.1.call-start
  16.3 60.2 %reduce-scatter.2.cloned.1.call-done = f32[16,16,128]{2,0,1:T(8,128)} async-done(((f32[256,16,128]{2,0,1:T(8,128)}), f32[16,16,128]{2,0,1:T(8,128)}) %reduce-scatter.2.cloned.1.call-update) | async-done | bytes 131088 | tf_op jit(solution)/shard_map/reduce_scatter | solution.py:36
  76.6 1.6 %copy.16 = f32[2,8,16,128]{3,1,2,0:T(8,128)} copy(f32[2,8,16,128]{3,2,1,0:T(8,128)} %bitcast.20) | data formatting | bytes 262144
  78.2 0.0 all-gather.2.cloned.1.call-update
  78.2 0.0 copy-done
  78.2 51.4 %all-gather.2.cloned.1.call-done = f32[256,2048]{1,0:T(8,128)} async-done(((f32[16,2048]{1,0:T(8,128)}), f32[256,2048]{1,0:T(8,128)}) %all-gather.2.cloned.1.call-update) | async-done | bytes 2097168 | tf_op jit(solution)/shard_map/all_gather | solution.py:47
  129.6 3.0 %fusion.7 = f32[16,2048]{1,0:T(8,128)} fusion(f32[256,2048]{1,0:T(8,128)} %all-gather.2.cloned.1.call-done, s32[256]{0:T(256)S(1)} %broadcast_subtract_fusion), kind=kOutput, calls=%fused_computation.11 | convolution fusion | flops 100667392 | bytes 2229248 | tf_op jit(solution)/shard_map/dot_general | solution.py:45
  (3 shorter events, 0.0 us)
Async XLA Ops:
  6.5 70.0 %reduce-scatter.2.cloned.1.call-start = ((), (), s32[]{:S(2)}) async-start(), calls=%async_computation.1 | async-start | bytes 2228224 | tf_op jit(solution)/shard_map/reduce_scatter | solution.py:36
  13.7 64.5 %copy-start = (s32[256]{0:T(256)S(1)}, s32[256]{0:T(256)}, u32[]{:S(2)}) copy-start(s32[256]{0:T(256)} %param.13) | copy-start | bytes 3076
  16.3 113.3 %all-gather.2.cloned.1.call-start = ((), (), s32[]{:S(2)}) async-start(), calls=%async_computation.2 | async-start | bytes 2228224 | tf_op jit(solution)/shard_map/all_gather | solution.py:47
Sparse Core Ops, SparseCore 0:
  16.4 60.1 reduce-scatter.1
  79.0 50.5 all-gather.1
where the time goes:
time: 140 us; the launch traced here: 139 us
  waiting for transfers between devices  112 us (80%)
  between operations  14.1 us (10%)
  matrix products  8.91 us (6%)
  other arithmetic  2.91 us (2%)
  local copies, waits for them, and re-layouts  1.84 us (1%)
    reduce_scatter x1, waiting for transfers between devices, body(): lax.psum_scatter(summed.reshape(lax.axis_size('scen') * own_blocks, KC, w...  60.2 us
    all_gather x1, waiting for transfers between devices, body(): lax.all_gather(reduced, 'clus', axis=0, tiled=True)  51.4 us
    dot_general x1, matrix products, body(): jnp.einsum('plqv,plq->plv', blocks, weighted_duals, preferred_element_typ...  3.37 us
    dot_general x1, matrix products, body(): jnp.dot(onehot, lax.all_gather(reduced, 'clus', axis=0, tiled=True), prec...  3.02 us
  transfers between devices with their start and end apart: 2, of which 2 were waited for; matrix products, arithmetic and copies ran while one was open for 0% of the time, Pallas kernels for 0%

commit v1 on v0

--- a/solution.py
+++ b/solution.py
@@ -44,7 +44,9 @@
     onehot = (owners[None, :] == jnp.arange(KC, dtype=jnp.int32)[:, None]).astype(jnp.float32)
     return jnp.dot(
         onehot,
-        lax.all_gather(reduced, "clus", axis=0, tiled=True),
+        jnp.concatenate(
+            lax.all_to_all(jnp.stack([reduced] * lax.axis_size("clus")), "clus", 0, 0), axis=0
+        ),
         precision=lax.Precision.HIGHEST,
         preferred_element_type=jnp.float32,
     )

time: 140 us -> 125 us (0.89)
  the two profiles are of different devices: /device:TPU:1 before, /device:TPU:225 now
where the time goes in v1:
time: 125 us
  waiting for transfers between devices  91.5 us (73%)
  between operations  14.1 us (11%)
  matrix products  7.3 us (6%)
  starting transfers between devices  6.64 us (5%)
  other arithmetic  2.91 us (2%)
  local copies, waits for them, and re-layouts  2.76 us (2%)
    reduce_scatter x1, waiting for transfers between devices, body(): lax.psum_scatter(summed.reshape(lax.axis_size('scen') * own_blocks, KC, w...  57.3 us
    all_to_all x1, waiting for transfers between devices, body(): lax.all_to_all(jnp.stack([reduced] * lax.axis_size('clus')), 'clus', 0, 0)  34.2 us
    all_to_all x1, starting transfers between devices, body(): lax.all_to_all(jnp.stack([reduced] * lax.axis_size('clus')), 'clus', 0, 0)  6.64 us
    dot_general x1, matrix products, body(): jnp.einsum('plqv,plq->plv', blocks, weighted_duals, preferred_element_typ...  3.37 us
  transfers between devices with their start and end apart: 2, of which 2 were waited for; matrix products, arithmetic and copies ran while one was open for 0% of the time, Pallas kernels for 0%

profile of v1, /device:TPU:225, one launch (start us, length us, event | category | flops | bytes accessed | tf_op | source)
XLA Modules:
  0.0 125.2 jit_solution(16346586638665970043)
XLA Ops:
  6.5 0.0 reduce-scatter.2.cloned.1.call-start
  7.2 0.7 broadcast_multiply_fusion
  7.9 0.7 broadcast_add_fusion
  8.5 0.1 copy.9
  8.6 0.1 reshape.88
  8.8 0.7 compare_select_fusion
  9.5 0.9 fusion.6
  10.3 3.4 %fusion.4 = f32[64,2,1,128]{3,2,1,0:T(1,128)S(1)} fusion(bf16[64,2,128,128]{3,2,1,0:T(8,128)(2,1)} %param.8, bf16[64,2,128,1]{2,1,0,3:T(2,128)(2,1)S(1)} %fusion.6), kind=kOutput, calls=%fused_computation.5 | convolution fusion | flops 4194304 | bytes 4292608 | tf_op jit(solution)/shard_map/plqv,plq->plv/dot_general | solution.py:20
  13.7 2.5 %fusion = f32[256,16,128]{2,0,1:T(8,128)} fusion(f32[128,128,1]{1,0,2:T(8,128)S(1)} %bitcast.21, s32[256,16]{0,1:T(8,128)S(1)} %multiply_add_fusion, s32[128]{0:T(128)S(1)} %and_select_fusion.1), kind=kOutput, calls=%fused_computation | convolution fusion | flops 805830656 | bytes 2179584 | tf_op jit(solution)/shard_map/dot_general | solution.py:33
  16.2 0.0 reduce-scatter.2.cloned.1.call-update
  16.2 57.3 %reduce-scatter.2.cloned.1.call-done = f32[16,16,128]{2,0,1:T(8,128)} async-done(((f32[256,16,128]{2,0,1:T(8,128)}), f32[16,16,128]{2,0,1:T(8,128)}) %reduce-scatter.2.cloned.1.call-update) | async-done | bytes 131088 | tf_op jit(solution)/shard_map/reduce_scatter | solution.py:36
  73.5 0.9 copy.16
  74.4 1.6 %stack.3 = f32[16,16,2048]{2,1,0:T(8,128)} broadcast(f32[16,2048]{1,0:T(8,128)S(1)} %bitcast.20), dimensions={1,2} | broadcast | bytes 2228224 | tf_op jit(solution)/shard_map/stack | solution.py:48
  76.0 0.0 copy-start
  76.0 6.6 %all-to-all-start = ((f32[16,16,2048]{2,1,0:T(8,128)}), f32[16,16,2048]{2,1,0:T(8,128)S(1)}, u32[]{:S(2)}, u32[]{:S(2)}) async-start(f32[16,16,2048]{2,1,0:T(8,128)} %stack.3), calls=%async_computation.1 | async-start | bytes 4194304 | tf_op jit(solution)/shard_map/all_to_all | solution.py:48
  82.7 0.0 copy-done
  82.7 34.2 %all-to-all-done = f32[16,16,2048]{2,1,0:T(8,128)S(1)} async-done(((f32[16,16,2048]{2,1,0:T(8,128)}), f32[16,16,2048]{2,1,0:T(8,128)S(1)}, u32[]{:S(2)}, u32[]{:S(2)}) %all-to-all-start) | async-done | bytes 2097184 | tf_op jit(solution)/shard_map/all_to_all | solution.py:48
  116.9 1.5 %fusion.7 = f32[16,2048]{1,0:T(8,128)} fusion(f32[256,2048]{1,0:T(8,128)S(1)} %bitcast.19, s32[256]{0:T(256)S(1)} %broadcast_subtract_fusion), kind=kOutput, calls=%fused_computation.11 | convolution fusion | flops 100667392 | bytes 2229248 | tf_op jit(solution)/shard_map/dot_general | solution.py:45
  (3 shorter events, 0.0 us)
Async XLA Ops:
  6.5 67.0 %reduce-scatter.2.cloned.1.call-start = ((), (), s32[]{:S(2)}) async-start(), calls=%async_computation.2 | async-start | bytes 2228224 | tf_op jit(solution)/shard_map/reduce_scatter | solution.py:36
  76.0 6.7 %copy-start = (s32[256]{0:T(256)S(1)}, s32[256]{0:T(256)}, u32[]{:S(2)}) copy-start(s32[256]{0:T(256)} %param.13) | copy-start | bytes 3076
  76.0 40.9 %all-to-all-start = ((f32[16,16,2048]{2,1,0:T(8,128)}), f32[16,16,2048]{2,1,0:T(8,128)S(1)}, u32[]{:S(2)}, u32[]{:S(2)}) async-start(f32[16,16,2048]{2,1,0:T(8,128)} %stack.3), calls=%async_computation.1 | async-start | bytes 4194304 | tf_op jit(solution)/shard_map/all_to_all | solution.py:48
Sparse Core Ops, SparseCore 0:
  16.3 57.0 reduce-scatter.1
